TPU v7x, 32 devices: a whole 2x2x4 slice. The times are simulated.
32 devices in a mesh: row: 8 (over z, core), col: 4 (over y, x).
Axes of the slice: x: 2, y: 2, z: 4, core: 2. Of those that a mesh axis runs over, the one named last changes fastest.
Arguments:
- tokens: bfloat16 [16384, 1024], P('row', 'col'), may hold values from -6 to 6
- memory: bfloat16 [4096, 1024], P('row', 'col'), may hold values from -6 to 6
- old_memory: bfloat16 [12288, 1024], P('row', 'col'), may hold values from -6 to 6
- doc_ids: int32 [8, 4096], P('row'), may hold values from 0 to 5, as said below
- norm_gains: bfloat16 [2, 1024], P(None, 'row'), may hold values from 0.5 to 1.5
- comp_weight: bfloat16 [3072, 1024], P('row', 'col'), may hold values from -0.109375 to 0.109375
- query_weight: bfloat16 [1024, 1024], P('row', 'col'), may hold values from -0.1875 to 0.1875
- key_weight: bfloat16 [1024, 1024], P('row', 'col'), may hold values from -0.1875 to 0.1875
- value_weight: bfloat16 [1024, 1024], P('row', 'col'), may hold values from -0.1875 to 0.1875
- proj_weight: bfloat16 [1024, 1024], P('col', 'row'), may hold values from -1.5 to 1.5
- up_weight: bfloat16 [1024, 4096], P('row', 'col'), may hold values from -0.1875 to 0.1875
- down_weight: bfloat16 [4096, 1024], P('col', 'row'), may hold values from -0.09375 to 0.09375
- cotangent: bfloat16 [16384, 1024], P('row', 'col'), may hold values from -6 to 6
Outputs:
- layer_out: bfloat16 [16384, 1024], P('row', 'col')
- grad_x: float32 [16384, 1024], P('row', 'col')
- grad_gains: float32 [2, 1024], P(None, 'row')
- grad_comp: float32 [3072, 1024], P('row', 'col')
- grad_query: float32 [1024, 1024], P('row', 'col')
- grad_key: float32 [1024, 1024], P('row', 'col')
- grad_value: float32 [1024, 1024], P('row', 'col')
- grad_proj: float32 [1024, 1024], P('col', 'row')
- grad_up: float32 [1024, 4096], P('row', 'col')
- grad_down: float32 [4096, 1024], P('col', 'row')
Inputs may be any that keep to these rules, and one draw needn't show every extreme that they name: In each row of doc_ids the numbers never fall and every number occurs; every document covers 200 entries or more.
All inputs are finite; a program needn't handle non-finite values.
Results may differ from a plain program's by a relative error of at most 0.015.
Values may be sent and summed in bfloat16 or wider, within the bound.
A program may use at most 192 MiB of HBM per device.

v0:
```python
import jax
import jax.numpy as jnp
from jax import lax
from jax.sharding import PartitionSpec as P

RATE = 3
HD = 128


def normalize(rows, gain):
    centre = rows - jnp.mean(rows, axis=-1, keepdims=True)
    spread = jnp.mean(centre * centre, axis=-1, keepdims=True)
    return centre * lax.rsqrt(spread + 1e-05) * gain


def contract_rows(left, right):
    return lax.dot_general(
        left, right, (((0,), (0,)), ((), ())), preferred_element_type=jnp.float32
    )


def contract_cols(left, right):
    return lax.dot_general(
        left, right, (((1,), (1,)), ((), ())), preferred_element_type=jnp.float32
    )


def on_device(
    tokens,
    memory,
    old_memory,
    doc_ids,
    norm_gains,
    comp_weight,
    query_weight,
    key_weight,
    value_weight,
    proj_weight,
    up_weight,
    down_weight,
    cotangent,
):
    full_tokens, full_memory, full_old, full_grad = (
        lax.all_gather(tokens, "col", axis=1, tiled=True),
        lax.all_gather(memory, "col", axis=1, tiled=True),
        lax.all_gather(old_memory, "col", axis=1, tiled=True),
        lax.all_gather(cotangent, "col", axis=1, tiled=True),
    )
    comp_full, query_full, key_full, value_full, up_full = (
        lax.all_gather(comp_weight, "row", axis=0, tiled=True),
        lax.all_gather(query_weight, "row", axis=0, tiled=True),
        lax.all_gather(key_weight, "row", axis=0, tiled=True),
        lax.all_gather(value_weight, "row", axis=0, tiled=True),
        lax.all_gather(up_weight, "row", axis=0, tiled=True),
    )
    proj_full, down_full, gain_full = (
        lax.all_gather(proj_weight, "row", axis=1, tiled=True),
        lax.all_gather(down_weight, "row", axis=1, tiled=True),
        lax.all_gather(norm_gains, "row", axis=1, tiled=True),
    )
    width = full_tokens.shape[1]
    slab = tokens.shape[1]
    column = lax.axis_index("col")
    seq_len = tokens.shape[0]
    mem_len = memory.shape[0]
    comp_len = old_memory.shape[0] // RATE
    start_tok = comp_len + mem_len
    all_keys = start_tok + seq_len
    gain_one = gain_full[0].astype(jnp.float32)
    gain_two = gain_full[1].astype(jnp.float32)
    old_rows = full_old.reshape(comp_len, RATE * width)
    compressed = jnp.dot(old_rows, comp_full, preferred_element_type=jnp.float32).astype(
        jnp.bfloat16
    )
    compressed_all = lax.all_gather(compressed, "col", axis=1, tiled=True)
    stacked = jnp.concatenate([compressed_all, full_memory, full_tokens], axis=0).astype(
        jnp.float32
    )
    normed = normalize(stacked, gain_one).astype(jnp.bfloat16)
    queries = jnp.dot(normed[start_tok:], query_full, preferred_element_type=jnp.float32).astype(
        jnp.bfloat16
    )
    keys = jnp.dot(normed, key_full, preferred_element_type=jnp.float32).astype(jnp.bfloat16)
    values = jnp.dot(normed, value_full, preferred_element_type=jnp.float32).astype(jnp.bfloat16)
    local_heads = queries.shape[1] // HD
    key_heads = keys.reshape(all_keys, local_heads, HD)
    value_heads = values.reshape(all_keys, local_heads, HD)
    doc_row = doc_ids[0]
    key_doc = jnp.concatenate(
        [doc_row[RATE - 1 : RATE * comp_len : RATE], doc_row[RATE * comp_len :]]
    )
    key_place = jnp.arange(all_keys, dtype=jnp.int32) - start_tok
    query_doc = doc_row[RATE * comp_len + mem_len :]
    query_place = jnp.arange(seq_len, dtype=jnp.int32)
    block = min(512, seq_len)
    steps_count = seq_len // block
    scale = HD ** (-0.5)
    query_blocks = queries.reshape(steps_count, block, local_heads, HD)
    doc_blocks = query_doc.reshape(steps_count, block)
    place_blocks = query_place.reshape(steps_count, block)

    def masked_scores(query_block, doc_block, place_block):
        allowed = (doc_block[:, None] == key_doc[None, :]) & (
            key_place[None, :] <= place_block[:, None]
        )
        scores = (
            jnp.einsum("qhd,khd->hqk", query_block, key_heads, preferred_element_type=jnp.float32)
            * scale
        )
        return jnp.where(allowed[None], scores, -1e30)

    def forward_block(items):
        query_block, doc_block, place_block = items
        scores = masked_scores(query_block, doc_block, place_block)
        top = jnp.max(scores, axis=-1, keepdims=True)
        raw = jnp.exp(scores - top)
        total = jnp.sum(raw, axis=-1, keepdims=True)
        rounded = (raw / total).astype(jnp.bfloat16)
        mixed_block = jnp.einsum(
            "hqk,khd->qhd", rounded, value_heads, preferred_element_type=jnp.float32
        )
        return (mixed_block, top, total)

    mixed_blocks, tops, totals = lax.map(forward_block, (query_blocks, doc_blocks, place_blocks))
    mixed = mixed_blocks.reshape(seq_len, local_heads * HD).astype(jnp.bfloat16)
    branch = lax.psum(jnp.dot(mixed, proj_full, preferred_element_type=jnp.float32), "col")
    resid = full_tokens.astype(jnp.float32) + branch
    hidden_in = normalize(resid, gain_two).astype(jnp.bfloat16)
    upper = jnp.dot(hidden_in, up_full, preferred_element_type=jnp.float32)
    active = jax.nn.gelu(upper).astype(jnp.bfloat16)
    down_terms = jnp.dot(active, down_full, preferred_element_type=jnp.float32)
    final = resid + lax.psum(down_terms.astype(jnp.bfloat16), "col").astype(jnp.float32)
    layer_out = lax.dynamic_slice_in_dim(final, column * slab, slab, 1).astype(jnp.bfloat16)
    grad_down = contract_rows(active, full_grad)
    grad_active = contract_cols(full_grad, down_full)
    _, gelu_pull = jax.vjp(jax.nn.gelu, upper)
    grad_upper = gelu_pull(grad_active)[0].astype(jnp.bfloat16)
    grad_up = contract_rows(hidden_in, grad_upper)
    grad_hidden = lax.psum(contract_cols(grad_upper, up_full), "col")
    _, second_pull = jax.vjp(normalize, resid, gain_two)
    grad_resid_norm, grad_gain_two = second_pull(grad_hidden)
    grad_resid = full_grad.astype(jnp.float32) + grad_resid_norm
    grad_branch = grad_resid.astype(jnp.bfloat16)
    grad_proj = contract_rows(mixed, grad_branch)
    grad_mixed = contract_cols(grad_branch, proj_full).astype(jnp.bfloat16)
    grad_blocks = grad_mixed.reshape(steps_count, block, local_heads, HD)

    def backward_block(carry, items):
        grad_keys, grad_values = carry
        query_block, doc_block, place_block, top, total, grad_out = items
        scores = masked_scores(query_block, doc_block, place_block)
        probs = jnp.exp(scores - top) / total
        rounded = probs.astype(jnp.bfloat16)
        grad_probs = jnp.einsum(
            "qhd,khd->hqk", grad_out, value_heads, preferred_element_type=jnp.float32
        )
        grad_scores = (
            probs * (grad_probs - jnp.sum(probs * grad_probs, axis=-1, keepdims=True))
        ).astype(jnp.bfloat16)
        grad_query_block = (
            jnp.einsum("hqk,khd->qhd", grad_scores, key_heads, preferred_element_type=jnp.float32)
            * scale
        )
        grad_keys = (
            grad_keys
            + jnp.einsum(
                "hqk,qhd->khd", grad_scores, query_block, preferred_element_type=jnp.float32
            )
            * scale
        )
        grad_values = grad_values + jnp.einsum(
            "hqk,qhd->khd", rounded, grad_out, preferred_element_type=jnp.float32
        )
        return ((grad_keys, grad_values), grad_query_block)

    empty = jnp.zeros((all_keys, local_heads, HD), jnp.float32)
    (grad_key_heads, grad_value_heads), grad_query_blocks = lax.scan(
        backward_block,
        (empty, empty),
        (query_blocks, doc_blocks, place_blocks, tops, totals, grad_blocks),
    )
    grad_queries = grad_query_blocks.reshape(seq_len, local_heads * HD).astype(jnp.bfloat16)
    grad_keys_low = grad_key_heads.reshape(all_keys, local_heads * HD).astype(jnp.bfloat16)
    grad_values_low = grad_value_heads.reshape(all_keys, local_heads * HD).astype(jnp.bfloat16)
    grad_query = contract_rows(normed[start_tok:], grad_queries)
    grad_key = contract_rows(normed, grad_keys_low)
    grad_value = contract_rows(normed, grad_values_low)
    back_keys = contract_cols(grad_keys_low, key_full) + contract_cols(grad_values_low, value_full)
    back_queries = contract_cols(grad_queries, query_full)
    partial_rows = jnp.concatenate(
        [back_keys[:start_tok], back_keys[start_tok:] + back_queries], axis=0
    )
    grad_normed = lax.psum(partial_rows, "col")
    _, first_pull = jax.vjp(normalize, stacked, gain_one)
    grad_stacked, grad_gain_one = first_pull(grad_normed)
    grad_comp_slab = lax.dynamic_slice_in_dim(grad_stacked[:comp_len], column * slab, slab, 1)
    grad_tok_slab = lax.dynamic_slice_in_dim(grad_stacked[start_tok:], column * slab, slab, 1)
    grad_x = lax.dynamic_slice_in_dim(grad_resid, column * slab, slab, 1) + grad_tok_slab
    grad_comp_low = grad_comp_slab.astype(jnp.bfloat16)
    grad_comp = contract_rows(old_rows, grad_comp_low)
    grad_gains = jnp.stack([grad_gain_one, grad_gain_two], axis=0)
    comp_part, query_part, key_part, value_part, up_part = (
        lax.psum_scatter(grad_comp, "row", scatter_dimension=0, tiled=True),
        lax.psum_scatter(grad_query, "row", scatter_dimension=0, tiled=True),
        lax.psum_scatter(grad_key, "row", scatter_dimension=0, tiled=True),
        lax.psum_scatter(grad_value, "row", scatter_dimension=0, tiled=True),
        lax.psum_scatter(grad_up, "row", scatter_dimension=0, tiled=True),
    )
    proj_part, down_part, gains_part = (
        lax.psum_scatter(grad_proj, "row", scatter_dimension=1, tiled=True),
        lax.psum_scatter(grad_down, "row", scatter_dimension=1, tiled=True),
        lax.psum_scatter(grad_gains, "row", scatter_dimension=1, tiled=True),
    )
    return (
        layer_out,
        grad_x,
        gains_part,
        comp_part,
        query_part,
        key_part,
        value_part,
        proj_part,
        up_part,
        down_part,
    )


def solution(mesh):
    in_specs = (
        P("row", "col"),
        P("row", "col"),
        P("row", "col"),
        P("row", None),
        P(None, "row"),
        P("row", "col"),
        P("row", "col"),
        P("row", "col"),
        P("row", "col"),
        P("col", "row"),
        P("row", "col"),
        P("col", "row"),
        P("row", "col"),
    )
    out_specs = (
        P("row", "col"),
        P("row", "col"),
        P(None, "row"),
        P("row", "col"),
        P("row", "col"),
        P("row", "col"),
        P("row", "col"),
        P("col", "row"),
        P("row", "col"),
        P("col", "row"),
    )
    return jax.shard_map(
        on_device, mesh=mesh, in_specs=in_specs, out_specs=out_specs, check_vma=False
    )
```

profile of v0, /device:TPU:0, one launch (start us, length us, event | category | flops | bytes accessed | tf_op | source)
XLA Modules:
  0.0 1541.5 jit_solution(4942058512463735601)
XLA Ops:
  10.1 46.2 %all-gather.11.cloned.1.call-done = bf16[1536,1024]{1,0:T(8,128)(2,1)} async-done(((bf16[1536,256]{1,0:T(8,128)(2,1)}), bf16[1536,1024]{1,0:T(8,128)(2,1)}) %all-gather.11.cloned.1.call-update) | async-done | bytes 3145744 | tf_op jit(solution)/shard_map/all_gather | solution.py:46
  60.6 22.7 %all-gather.13.cloned.1.call-done = bf16[3072,256]{1,0:T(8,128)(2,1)} async-done(((bf16[384,256]{1,0:T(8,128)(2,1)}), bf16[3072,256]{1,0:T(8,128)(2,1)}) %all-gather.13.cloned.1.call-update) | async-done | bytes 1572880 | tf_op jit(solution)/shard_map/all_gather | solution.py:50
  88.0 9.9 all_gather.44
  98.6 15.8 %all_gather.45 = bf16[1024,256]{1,0:T(8,128)(2,1)} all-gather(bf16[128,256]{1,0:T(8,128)(2,1)S(1)} %copy-done.47), channel_id=1, replica_groups=mesh['row'=8,'col'=4] {'row'}, dimensions={0}, use_global_device_ids=true | all-gather | bytes 589824 | tf_op jit(solution)/shard_map/all_gather | solution.py:51
  114.4 15.8 %all_gather.46 = bf16[1024,256]{1,0:T(8,128)(2,1)} all-gather(bf16[128,256]{1,0:T(8,128)(2,1)S(1)} %copy-done.48), channel_id=1, replica_groups=mesh['row'=8,'col'=4] {'row'}, dimensions={0}, use_global_device_ids=true | all-gather | bytes 589824 | tf_op jit(solution)/shard_map/all_gather | solution.py:52
  130.2 15.8 %all_gather.47 = bf16[1024,256]{1,0:T(8,128)(2,1)} all-gather(bf16[128,256]{1,0:T(8,128)(2,1)S(1)} %copy-done.49), channel_id=1, replica_groups=mesh['row'=8,'col'=4] {'row'}, dimensions={0}, use_global_device_ids=true | all-gather | bytes 589824 | tf_op jit(solution)/shard_map/all_gather | solution.py:53
  146.1 15.2 all_gather.48
  164.8 28.6 %all-gather.15.cloned.1.call-done = bf16[512,1024]{1,0:T(8,128)(2,1)} async-done(((bf16[512,256]{1,0:T(8,128)(2,1)}), bf16[512,1024]{1,0:T(8,128)(2,1)}) %all-gather.15.cloned.1.call-update) | async-done | bytes 1048592 | tf_op jit(solution)/shard_map/all_gather | solution.py:75
  232.0 61.1 %while.30 = (s32[]{:T(128)}, bf16[4,512,2,128]{3,1,2,0:T(8,128)(2,1)}, f32[4,2,512,1]{2,1,3,0:T(2,128)S(1)}, f32[4,2,512,1]{2,1,3,0:T(2,128)S(1)}, s32[4,512]{1,...) while((s32[]{:T(128)}, ...), condition=%wide.region_5.6_spmd.clone, body=%wide.region_2.5_spmd.clone.sunk | while | flops 1653081088 | bytes 56447168 | solution.py:124
  303.6 10.7 fusion.78
  314.3 160.6 %all-reduce.5.cloned.1.call-done = f32[2048,1024]{1,0:T(8,128)} async-done(((f32[2048,1024]{1,0:T(8,128)}), f32[2048,1024]{1,0:T(8,128)}) %all-reduce.5.cloned.1.call-update) | async-done | bytes 8388624 | tf_op jit(solution)/shard_map/psum | solution.py:126
  486.3 20.1 %all-gather.19.cloned.1.call-done = bf16[1024,1024]{1,0:T(8,128)(2,1)} async-done(((bf16[128,1024]{1,0:T(8,128)(2,1)}), bf16[1024,1024]{1,0:T(8,128)(2,1)}) %all-gather.19.cloned.1.call-update) | async-done | bytes 2097168 | tf_op jit(solution)/shard_map/all_gather | solution.py:54
  506.4 16.1 %fusion.50 = (bf16[2048,1024]{1,0:T(8,128)(2,1)S(1)}, f32[2048,1024]{1,0:T(8,128)}) fusion(f32[2048,1024]{1,0:T(8,128)} %fusion.78, bf16[2048,1024]{1,0:T(8,128)(2,1)} %multiply_convert_fusion.2, bf16[1024,1024]{1,0:T(8,128)(2,1)} %all-gather.19.cloned.1.call-done), kind=kOutput, calls=%fused_computation.73 | convolution fusion | flops 4336910336 | bytes 27262976 | tf_op jit(solution)/shard_map/dot_general | solution.py:129
  531.6 171.5 %all-reduce.9.cloned.1.call-done = f32[2048,1024]{1,0:T(8,128)} async-done(((f32[2048,1024]{1,0:T(8,128)}), f32[2048,1024]{1,0:T(8,128)}) %all-reduce.9.cloned.1.call-update) | async-done | bytes 8388624 | tf_op jit(solution)/shard_map/psum | solution.py:139
  726.2 122.1 %while.31 = (s32[]{:T(128)}, f32[3072,2,128]{0,2,1:T(8,128)S(1)}, f32[3072,2,128]{0,2,1:T(8,128)}, bf16[4,512,2,128]{3,1,2,0:T(8,128)(2,1)}, bf16[4,512,2,128]{3...) while((s32[]{:T(128)}, f32[3072,2,128]{0,2,1:T(8,128)S(1)}, ...), condition=%wide.region_15.16_spmd.clone, body=%wide.region_13.15_spmd.clone.sunk | while | flops 4066772992 | bytes 161038704 | solution.py:177
  863.4 11.9 pad_maximum_fusion
  875.6 11.8 convolution_convert_fusion.2
  887.5 227.9 %all-reduce.11.cloned.1.call-done = f32[3072,1024]{1,0:T(8,128)} async-done(((f32[3072,1024]{1,0:T(8,128)}), f32[3072,1024]{1,0:T(8,128)}) %all-reduce.11.cloned.1.call-update) | async-done | bytes 12582928 | tf_op jit(solution)/shard_map/psum | solution.py:193
  1115.5 9.9 fusion.43
  1126.9 11.9 fusion.41
  1139.9 11.5 broadcast_add_fusion
  1161.4 10.2 fusion.83
  1171.6 12.3 fusion.74
  1206.9 15.3 all-reduce.7.cloned.1.call-done
  1232.0 23.9 %reduce-scatter.25.cloned.1.call-done = f32[128,2]{1,0:T(8,128)} async-done(((f32[1024,2]{1,0:T(8,128)}), f32[128,2]{1,0:T(8,128)}) %reduce-scatter.25.cloned.1.call-update) | async-done | bytes 1040
  1257.4 39.2 %reduce-scatter.11.cloned.1.call-done = f32[384,256]{0,1:T(8,128)} async-done(((f32[3072,256]{0,1:T(8,128)}), f32[384,256]{0,1:T(8,128)}) %reduce-scatter.11.cloned.1.call-update) | async-done | bytes 393232 | tf_op jit(solution)/shard_map/reduce_scatter | solution.py:203
  1298.6 50.2 %reduce-scatter.21.cloned.1.call-done = f32[128,1024]{1,0:T(8,128)} async-done(((f32[1024,1024]{1,0:T(8,128)}), f32[128,1024]{1,0:T(8,128)}) %reduce-scatter.21.cloned.1.call-update) | async-done | bytes 524304 | tf_op jit(solution)/shard_map/reduce_scatter | solution.py:207
  1348.7 51.1 %reduce-scatter.23.cloned.1.call-done = f32[1024,128]{1,0:T(8,128)} async-done(((f32[1024,1024]{1,0:T(8,128)}), f32[1024,128]{1,0:T(8,128)}) %reduce-scatter.23.cloned.1.call-update) | async-done | bytes 524304 | tf_op jit(solution)/shard_map/reduce_scatter | solution.py:211
  1399.8 33.8 %reduce-scatter.19.cloned.1.call-done = f32[256,128]{1,0:T(8,128)} async-done(((f32[256,1024]{1,0:T(8,128)}), f32[256,128]{1,0:T(8,128)}) %reduce-scatter.19.cloned.1.call-update) | async-done | bytes 131088 | tf_op jit(solution)/shard_map/reduce_scatter | solution.py:210
  1433.7 33.6 %reduce-scatter.13.cloned.1.call-done = f32[128,256]{1,0:T(8,128)} async-done(((f32[1024,256]{1,0:T(8,128)}), f32[128,256]{1,0:T(8,128)}) %reduce-scatter.13.cloned.1.call-update) | async-done | bytes 131088 | tf_op jit(solution)/shard_map/reduce_scatter | solution.py:204
  1467.2 33.8 %reduce-scatter.15.cloned.1.call-done = f32[128,256]{1,0:T(8,128)} async-done(((f32[1024,256]{1,0:T(8,128)}), f32[128,256]{1,0:T(8,128)}) %reduce-scatter.15.cloned.1.call-update) | async-done | bytes 131088 | tf_op jit(solution)/shard_map/reduce_scatter | solution.py:205
  1501.0 33.5 %reduce-scatter.17.cloned.1.call-done = f32[128,256]{1,0:T(8,128)} async-done(((f32[1024,256]{1,0:T(8,128)}), f32[128,256]{1,0:T(8,128)}) %reduce-scatter.17.cloned.1.call-update) | async-done | bytes 131088 | tf_op jit(solution)/shard_map/reduce_scatter | solution.py:206
  (347 shorter events, 353.9 us)
Async XLA Ops:
  7.2 91.4 %copy-start.47 = (bf16[128,256]{1,0:T(8,128)(2,1)S(1)}, bf16[128,256]{1,0:T(8,128)(2,1)}, u32[]{:S(2)}) copy-start(bf16[128,256]{1,0:T(8,128)(2,1)} %param.23) | copy-start | bytes 196612
  7.2 107.2 %copy-start.48 = (bf16[128,256]{1,0:T(8,128)(2,1)S(1)}, bf16[128,256]{1,0:T(8,128)(2,1)}, u32[]{:S(2)}) copy-start(bf16[128,256]{1,0:T(8,128)(2,1)} %param.24) | copy-start | bytes 196612
  7.2 49.1 %all-gather.11.cloned.1.call-start = ((), (), s32[]{:S(2)}) async-start(), calls=%async_computation.9 | async-start | bytes 3932160 | tf_op jit(solution)/shard_map/all_gather | solution.py:46
  8.0 122.3 %copy-start.49 = (bf16[128,256]{1,0:T(8,128)(2,1)S(1)}, bf16[128,256]{1,0:T(8,128)(2,1)}, u32[]{:S(2)}) copy-start(bf16[128,256]{1,0:T(8,128)(2,1)} %param.25) | copy-start | bytes 196612
  8.0 75.3 %all-gather.13.cloned.1.call-start = ((), (), s32[]{:S(2)}) async-start(), calls=%async_computation.10 | async-start | bytes 1769472 | tf_op jit(solution)/shard_map/all_gather | solution.py:50
  8.7 152.6 %all-gather.17.cloned.1.call-start = ((), (), s32[]{:S(2)}) async-start(), calls=%async_computation.12 | async-start | bytes 1310720 | tf_op jit(solution)/shard_map/all_gather | solution.py:45
  9.4 136.6 %copy-start.50 = (bf16[256,128]{1,0:T(8,128)(2,1)S(1)}, bf16[256,128]{1,0:T(8,128)(2,1)}, u32[]{:S(2)}) copy-start(bf16[256,128]{1,0:T(8,128)(2,1)} %param.26) | copy-start | bytes 196612
  9.5 155.3 %all-gather.9.cloned.1.call-start = ((), (), s32[]{:S(2)}) async-start(), calls=%async_computation.8 | async-start | bytes 5242880 | tf_op jit(solution)/shard_map/all_gather | solution.py:44
  10.0 183.4 %all-gather.15.cloned.1.call-start = ((), (), s32[]{:S(2)}) async-start(), calls=%async_computation.11 | async-start | bytes 1310720 | tf_op jit(solution)/shard_map/all_gather | solution.py:75
  60.5 100.8 %copy-start.19 = (bf16[512,3072]{1,0:T(8,128)(2,1)}, bf16[512,3072]{1,0:T(8,128)(2,1)S(1)}, u32[]{:S(2)}) copy-start(bf16[512,3072]{1,0:T(8,128)(2,1)S(1)} %reshape.251) | copy-start | bytes 9437188
  86.4 217.2 %all-gather.21.cloned.1.call-start = ((), (), s32[]{:S(2)}) async-start(), calls=%async_computation.15 | async-start | bytes 2359296 | tf_op jit(solution)/shard_map/all_gather | solution.py:58
  86.9 216.6 %all-gather.23.cloned.1.call-start = ((), (), s32[]{:S(2)}) async-start(), calls=%async_computation.17 | async-start | bytes 5242880 | tf_op jit(solution)/shard_map/all_gather | solution.py:47
  87.7 387.2 %all-reduce.5.cloned.1.call-start = ((), (), s32[]{:S(2)}) async-start(), calls=%async_computation.13 | async-start | bytes 16777216 | tf_op jit(solution)/shard_map/psum | solution.py:126
  98.5 111.4 %copy-start.45 = (f32[1,1024]{1,0:T(1,128)}, f32[1,1024]{1,0:T(1,128)S(1)}, u32[]{:S(2)}) copy-start(f32[1,1024]{1,0:T(1,128)S(1)} %get-tuple-element.379) | copy-start | bytes 12292
  302.8 203.6 %all-gather.19.cloned.1.call-start = ((), (), s32[]{:S(2)}) async-start(), calls=%async_computation.14 | async-start | bytes 2359296 | tf_op jit(solution)/shard_map/all_gather | solution.py:54
  303.5 399.6 %all-reduce.9.cloned.1.call-start = ((), (), s32[]{:S(2)}) async-start(), calls=%async_computation.18 | async-start | bytes 16777216 | tf_op jit(solution)/shard_map/psum | solution.py:139
  531.5 583.9 %all-reduce.11.cloned.1.call-start = ((), (), s32[]{:S(2)}) async-start(), calls=%async_computation.19 | async-start | bytes 25165824 | tf_op jit(solution)/shard_map/psum | solution.py:193
  875.3 346.9 %all-reduce.7.cloned.1.call-start = ((), (), s32[]{:S(2)}) async-start(), calls=%async_computation.16 | async-start | bytes 8388608 | tf_op jit(solution)/shard_map/psum | solution.py:132
  875.6 239.9 %copy-start.13 = (bf16[512,1024]{1,0:T(8,128)(2,1)S(1)}, bf16[512,1024]{1,0:T(8,128)(2,1)}, u32[]{:S(2)}) copy-start(bf16[512,1024]{1,0:T(8,128)(2,1)} %all-gather.17.cloned.1.call-done) | copy-start | bytes 3145732
  875.6 239.9 %copy-start.15 = (bf16[512,1024]{1,0:T(8,128)(2,1)S(1)}, bf16[512,1024]{1,0:T(8,128)(2,1)}, u32[]{:S(2)}) copy-start(bf16[512,1024]{1,0:T(8,128)(2,1)} %all-gather.15.cloned.1.call-done) | copy-start | bytes 3145732
  875.6 239.9 %copy-start.40 = (f32[3072]{0:T(1024)S(1)}, f32[3072]{0:T(1024)}, u32[]{:S(2)}) copy-start(f32[3072]{0:T(1024)} %copy-done.39) | copy-start | bytes 36868
  875.6 239.9 %copy-start.46 = (f32[1,1024]{1,0:T(1,128)S(1)}, f32[1,1024]{1,0:T(1,128)}, u32[]{:S(2)}) copy-start(f32[1,1024]{1,0:T(1,128)} %copy-done.45) | copy-start | bytes 12292
  887.4 238.0 %copy-start.44 = (f32[3072]{0:T(1024)S(1)}, f32[3072]{0:T(1024)}, u32[]{:S(2)}) copy-start(f32[3072]{0:T(1024)} %copy-done.43) | copy-start | bytes 36868
  887.4 238.0 %copy-start.42 = (f32[3072]{0:T(1024)S(1)}, f32[3072]{0:T(1024)}, u32[]{:S(2)}) copy-start(f32[3072]{0:T(1024)} %copy-done.41) | copy-start | bytes 36868
  887.5 368.5 %reduce-scatter.25.cloned.1.call-start = ((), (), s32[]{:S(2)}) async-start(), calls=%async_computation.27 | async-start | bytes 589824
  1156.4 140.2 %reduce-scatter.11.cloned.1.call-start = ((), (), s32[]{:S(2)}) async-start(), calls=%async_computation.20 | async-start | bytes 3538944 | tf_op jit(solution)/shard_map/reduce_scatter | solution.py:203
  1161.1 187.7 %reduce-scatter.21.cloned.1.call-start = ((), (), s32[]{:S(2)}) async-start(), calls=%async_computation.25 | async-start | bytes 4718592 | tf_op jit(solution)/shard_map/reduce_scatter | solution.py:207
  1171.6 228.3 %reduce-scatter.23.cloned.1.call-start = ((), (), s32[]{:S(2)}) async-start(), calls=%async_computation.26 | async-start | bytes 4718592 | tf_op jit(solution)/shard_map/reduce_scatter | solution.py:211
  1183.9 249.7 %reduce-scatter.19.cloned.1.call-start = ((), (), s32[]{:S(2)}) async-start(), calls=%async_computation.24 | async-start | bytes 1179648 | tf_op jit(solution)/shard_map/reduce_scatter | solution.py:210
  1189.6 277.6 %reduce-scatter.13.cloned.1.call-start = ((), (), s32[]{:S(2)}) async-start(), calls=%async_computation.21 | async-start | bytes 1179648 | tf_op jit(solution)/shard_map/reduce_scatter | solution.py:204
  1194.6 306.4 %reduce-scatter.15.cloned.1.call-start = ((), (), s32[]{:S(2)}) async-start(), calls=%async_computation.22 | async-start | bytes 1179648 | tf_op jit(solution)/shard_map/reduce_scatter | solution.py:205
  1201.2 333.3 %reduce-scatter.17.cloned.1.call-start = ((), (), s32[]{:S(2)}) async-start(), calls=%async_computation.23 | async-start | bytes 1179648 | tf_op jit(solution)/shard_map/reduce_scatter | solution.py:206
  (70 other events, 565.9 us)
Sparse Core Ops, SparseCore 0:
  9.8 46.4 all-gather.10
  58.0 25.2 all-gather.12
  85.1 25.4 all-gather.16
  112.3 52.4 all-gather.8
  167.0 26.3 all-gather.14
  194.9 30.5 all-gather.20
  227.3 51.4 all-gather.22
  302.9 171.9 all-reduce.4
  476.5 29.8 all-gather.18
  531.6 171.4 all-reduce.8
  875.4 239.9 all-reduce.10
  1118.6 103.6 all-reduce.6
  1224.5 31.3 reduce-scatter.24
  1258.1 38.5 reduce-scatter.10
  1299.4 49.3 reduce-scatter.20
  1351.4 48.3 reduce-scatter.22
  1402.5 31.0 reduce-scatter.18
  1436.4 30.8 reduce-scatter.12
  1470.1 30.8 reduce-scatter.14
  1503.7 30.7 reduce-scatter.16
where the time goes:
time: 1550 us; the launch traced here: 1540 us
  waiting for transfers between devices  1000 us (65%)
  matrix products  250 us (16%)
  other arithmetic  142 us (9%)
  blocking collectives  72.7 us (5%)
  local copies, waits for them, and re-layouts  58.5 us (4%)
    psum x1, waiting for transfers between devices, on_device(): grad_normed = lax.psum(partial_rows, 'col')  228 us
    psum x1, waiting for transfers between devices, on_device(): grad_hidden = lax.psum(contract_cols(grad_upper, up_full), 'col')  172 us
    psum x1, waiting for transfers between devices, on_device(): lax.psum(jnp.dot(mixed, proj_full, preferred_element_type=jnp.float32), '...  161 us
    reduce_scatter x1, waiting for transfers between devices, on_device(): lax.psum_scatter(grad_down, 'row', scatter_dimension=1, tiled=True)  51.1 us
    reduce_scatter x1, waiting for transfers between devices, on_device(): lax.psum_scatter(grad_up, 'row', scatter_dimension=0, tiled=True)  50.2 us
    dot_general x8, matrix products, masked_scores(): jnp.einsum('qhd,khd->hqk', query_block, key_heads, preferred_element_type...  49.4 us
    dot_general x7, matrix products, contract_rows(): lax.dot_general(left, right, (((0,), (0,)), ((), ())), preferred_element_...  49.2 us
    all_gather x1, waiting for transfers between devices, on_device(): lax.all_gather(old_memory, 'col', axis=1, tiled=True)  46.2 us
  transfers between devices with their start and end apart: 20, of which 17 were waited for; matrix products, arithmetic and copies ran while one was open for 15% of the time, Pallas kernels for 0%

commit v1 on v0

--- a/solution.py
+++ b/solution.py
@@ -190,7 +190,14 @@
     partial_rows = jnp.concatenate(
         [back_keys[:start_tok], back_keys[start_tok:] + back_queries], axis=0
     )
-    grad_normed = lax.psum(partial_rows, "col")
+    k_all = lax.axis_size("col")
+    grad_normed = partial_rows
+    for hop_no in [m for m in (1, 2, 4, 8, 16) if m < k_all]:
+        series = []
+        for k0 in range(k_all):
+            series.append((k0, k0 ^ hop_no))
+        moved = lax.ppermute(grad_normed, "col", series)
+        grad_normed = grad_normed + moved
     _, first_pull = jax.vjp(normalize, stacked, gain_one)
     grad_stacked, grad_gain_one = first_pull(grad_normed)
     grad_comp_slab = lax.dynamic_slice_in_dim(grad_stacked[:comp_len], column * slab, slab, 1)

time: 1550 us -> 1860 us (1.20)
  waiting for transfers between devices: 1000 us -> 1300 us
    ppermute x0 -> x2, waiting for transfers between devices: none -> 596 us  [on_device(): moved = lax.ppermute(grad_normed, 'col', series)]
    psum x1 -> x0, waiting for transfers between devices: 228 us -> none  [on_device(): grad_normed = lax.psum(partial_rows, 'col')]
    reduce_scatter x1, waiting for transfers between devices: 39.2 us -> 12.2 us  [on_device(): lax.psum_scatter(grad_comp, 'row', scatter_dimension=0, tiled=True)]
    unnamed x21 -> x20, waiting for transfers between devices: 28.6 us -> 4.68 us
  transfers between devices with their start and end apart: 20 -> 21, of which waited for: 17 -> 16; matrix products, arithmetic and copies ran while one was open for 15% -> 13% of each run, Pallas kernels for 0% -> 0%
where the time goes in v1:
time: 1860 us
  waiting for transfers between devices  1300 us (70%)
  matrix products  248 us (13%)
  other arithmetic  160 us (9%)
  blocking collectives  72.7 us (4%)
  local copies, waits for them, and re-layouts  54.8 us (3%)
    ppermute x2, waiting for transfers between devices, on_device(): moved = lax.ppermute(grad_normed, 'col', series)  596 us
    psum x1, waiting for transfers between devices, on_device(): grad_hidden = lax.psum(contract_cols(grad_upper, up_full), 'col')  172 us
    psum x1, waiting for transfers between devices, on_device(): lax.psum(jnp.dot(mixed, proj_full, preferred_element_type=jnp.float32), '...  161 us
    reduce_scatter x1, waiting for transfers between devices, on_device(): lax.psum_scatter(grad_down, 'row', scatter_dimension=1, tiled=True)  51.1 us
    reduce_scatter x1, waiting for transfers between devices, on_device(): lax.psum_scatter(grad_up, 'row', scatter_dimension=0, tiled=True)  50 us
    dot_general x8, matrix products, masked_scores(): jnp.einsum('qhd,khd->hqk', query_block, key_heads, preferred_element_type...  49.3 us
    dot_general x7, matrix products, contract_rows(): lax.dot_general(left, right, (((0,), (0,)), ((), ())), preferred_element_...  48.2 us
    all_gather x1, waiting for transfers between devices, on_device(): lax.all_gather(old_memory, 'col', axis=1, tiled=True)  46.2 us
  transfers between devices with their start and end apart: 21, of which 16 were waited for; matrix products, arithmetic and copies ran while one was open for 13% of the time, Pallas kernels for 0%

profile of v1, /device:TPU:0, one launch (start us, length us, event | category | flops | bytes accessed | tf_op | source)
XLA Modules:
  0.0 1858.2 jit_solution(1335826131025404506)
XLA Ops:
  10.1 46.2 %all-gather.11.cloned.1.call-done = bf16[1536,1024]{1,0:T(8,128)(2,1)} async-done(((bf16[1536,256]{1,0:T(8,128)(2,1)}), bf16[1536,1024]{1,0:T(8,128)(2,1)}) %all-gather.11.cloned.1.call-update) | async-done | bytes 3145744 | tf_op jit(solution)/shard_map/all_gather | solution.py:46
  60.6 22.7 %all-gather.13.cloned.1.call-done = bf16[3072,256]{1,0:T(8,128)(2,1)} async-done(((bf16[384,256]{1,0:T(8,128)(2,1)}), bf16[3072,256]{1,0:T(8,128)(2,1)}) %all-gather.13.cloned.1.call-update) | async-done | bytes 1572880 | tf_op jit(solution)/shard_map/all_gather | solution.py:50
  88.0 9.9 all_gather.44
  98.6 15.8 all_gather.45
  114.4 15.8 all_gather.46
  130.2 15.8 all_gather.47
  146.1 15.2 all_gather.48
  164.8 28.6 %all-gather.15.cloned.1.call-done = bf16[512,1024]{1,0:T(8,128)(2,1)} async-done(((bf16[512,256]{1,0:T(8,128)(2,1)}), bf16[512,1024]{1,0:T(8,128)(2,1)}) %all-gather.15.cloned.1.call-update) | async-done | bytes 1048592 | tf_op jit(solution)/shard_map/all_gather | solution.py:75
  232.0 61.1 %while.30 = (s32[]{:T(128)}, bf16[4,512,2,128]{3,1,2,0:T(8,128)(2,1)}, f32[4,2,512,1]{2,1,3,0:T(2,128)S(1)}, f32[4,2,512,1]{2,1,3,0:T(2,128)S(1)}, s32[4,512]{1,...) while((s32[]{:T(128)}, ...), condition=%wide.region_5.6_spmd.clone, body=%wide.region_2.5_spmd.clone.sunk | while | flops 1653081088 | bytes 56447168 | solution.py:124
  303.6 10.7 fusion.79
  314.4 160.5 %all-reduce.4.cloned.1.call-done = f32[2048,1024]{1,0:T(8,128)} async-done(((f32[2048,1024]{1,0:T(8,128)}), f32[2048,1024]{1,0:T(8,128)}) %all-reduce.4.cloned.1.call-update) | async-done | bytes 8388624 | tf_op jit(solution)/shard_map/psum | solution.py:126
  486.3 20.1 %all-gather.19.cloned.1.call-done = bf16[1024,1024]{1,0:T(8,128)(2,1)} async-done(((bf16[128,1024]{1,0:T(8,128)(2,1)}), bf16[1024,1024]{1,0:T(8,128)(2,1)}) %all-gather.19.cloned.1.call-update) | async-done | bytes 2097168 | tf_op jit(solution)/shard_map/all_gather | solution.py:54
  506.4 16.0 fusion.50
  531.4 171.5 %all-reduce.8.cloned.1.call-done = f32[2048,1024]{1,0:T(8,128)} async-done(((f32[2048,1024]{1,0:T(8,128)}), f32[2048,1024]{1,0:T(8,128)}) %all-reduce.8.cloned.1.call-update) | async-done | bytes 8388624 | tf_op jit(solution)/shard_map/psum | solution.py:139
  726.0 122.1 %while.31 = (s32[]{:T(128)}, f32[3072,2,128]{0,2,1:T(8,128)S(1)}, f32[3072,2,128]{0,2,1:T(8,128)}, bf16[4,512,2,128]{3,1,2,0:T(8,128)(2,1)}, bf16[4,512,2,128]{3...) while((s32[]{:T(128)}, f32[3072,2,128]{0,2,1:T(8,128)S(1)}, ...), condition=%wide.region_15.16_spmd.clone, body=%wide.region_13.15_spmd.clone.sunk | while | flops 4066772992 | bytes 161038704 | solution.py:177
  863.1 12.0 pad_maximum_fusion
  876.6 270.6 %collective-permute-done = f32[3072,1024]{1,0:T(8,128)S(1)} collective-permute-done((f32[3072,1024]{1,0:T(8,128)}, f32[3072,1024]{1,0:T(8,128)S(1)}, u32[]{:S(2)}, u32[]{:S(2)}) %collective-permute-start) | collective-permute-done | bytes 12582944 | tf_op jit(solution)/shard_map/ppermute | solution.py:199
  1147.2 10.3 fusion.74
  1158.9 11.7 convolution_convert_fusion.2
  1170.7 325.7 %collective-permute-done.1 = f32[3072,1024]{1,0:T(8,128)} collective-permute-done((f32[3072,1024]{1,0:T(8,128)}, f32[3072,1024]{1,0:T(8,128)}, u32[]{:S(2)}, u32[]{:S(2)}) %collective-permute-start.1) | collective-permute-done | bytes 12582944 | tf_op jit(solution)/shard_map/ppermute | solution.py:199
  1496.4 13.3 fusion.41
  1510.7 17.2 fusion.76
  1527.9 10.3 broadcast_add_fusion
  1545.1 10.1 fusion.84
  1555.3 12.1 fusion.75
  1601.6 12.2 reduce-scatter.11.cloned.1.call-done
  1615.8 50.0 %reduce-scatter.21.cloned.1.call-done = f32[128,1024]{1,0:T(8,128)} async-done(((f32[1024,1024]{1,0:T(8,128)}), f32[128,1024]{1,0:T(8,128)}) %reduce-scatter.21.cloned.1.call-update) | async-done | bytes 524304 | tf_op jit(solution)/shard_map/reduce_scatter | solution.py:214
  1665.8 51.1 %reduce-scatter.23.cloned.1.call-done = f32[1024,128]{1,0:T(8,128)} async-done(((f32[1024,1024]{1,0:T(8,128)}), f32[1024,128]{1,0:T(8,128)}) %reduce-scatter.23.cloned.1.call-update) | async-done | bytes 524304 | tf_op jit(solution)/shard_map/reduce_scatter | solution.py:218
  1716.9 33.8 %reduce-scatter.19.cloned.1.call-done = f32[256,128]{1,0:T(8,128)} async-done(((f32[256,1024]{1,0:T(8,128)}), f32[256,128]{1,0:T(8,128)}) %reduce-scatter.19.cloned.1.call-update) | async-done | bytes 131088 | tf_op jit(solution)/shard_map/reduce_scatter | solution.py:217
  1750.7 33.7 %reduce-scatter.13.cloned.1.call-done = f32[128,256]{1,0:T(8,128)} async-done(((f32[1024,256]{1,0:T(8,128)}), f32[128,256]{1,0:T(8,128)}) %reduce-scatter.13.cloned.1.call-update) | async-done | bytes 131088 | tf_op jit(solution)/shard_map/reduce_scatter | solution.py:211
  1784.4 33.5 %reduce-scatter.15.cloned.1.call-done = f32[128,256]{1,0:T(8,128)} async-done(((f32[1024,256]{1,0:T(8,128)}), f32[128,256]{1,0:T(8,128)}) %reduce-scatter.15.cloned.1.call-update) | async-done | bytes 131088 | tf_op jit(solution)/shard_map/reduce_scatter | solution.py:212
  1817.9 33.6 %reduce-scatter.17.cloned.1.call-done = f32[128,256]{1,0:T(8,128)} async-done(((f32[1024,256]{1,0:T(8,128)}), f32[128,256]{1,0:T(8,128)}) %reduce-scatter.17.cloned.1.call-update) | async-done | bytes 131088 | tf_op jit(solution)/shard_map/reduce_scatter | solution.py:213
  (345 shorter events, 351.8 us)
Async XLA Ops:
  7.2 107.2 %copy-start.44 = (bf16[128,256]{1,0:T(8,128)(2,1)S(1)}, bf16[128,256]{1,0:T(8,128)(2,1)}, u32[]{:S(2)}) copy-start(bf16[128,256]{1,0:T(8,128)(2,1)} %param.24) | copy-start | bytes 196612
  7.2 49.1 %all-gather.11.cloned.1.call-start = ((), (), s32[]{:S(2)}) async-start(), calls=%async_computation.9 | async-start | bytes 3932160 | tf_op jit(solution)/shard_map/all_gather | solution.py:46
  8.0 122.3 %copy-start.45 = (bf16[128,256]{1,0:T(8,128)(2,1)S(1)}, bf16[128,256]{1,0:T(8,128)(2,1)}, u32[]{:S(2)}) copy-start(bf16[128,256]{1,0:T(8,128)(2,1)} %param.25) | copy-start | bytes 196612
  8.0 75.3 %all-gather.13.cloned.1.call-start = ((), (), s32[]{:S(2)}) async-start(), calls=%async_computation.10 | async-start | bytes 1769472 | tf_op jit(solution)/shard_map/all_gather | solution.py:50
  8.7 152.6 %all-gather.17.cloned.1.call-start = ((), (), s32[]{:S(2)}) async-start(), calls=%async_computation.12 | async-start | bytes 1310720 | tf_op jit(solution)/shard_map/all_gather | solution.py:45
  9.4 136.6 %copy-start.46 = (bf16[256,128]{1,0:T(8,128)(2,1)S(1)}, bf16[256,128]{1,0:T(8,128)(2,1)}, u32[]{:S(2)}) copy-start(bf16[256,128]{1,0:T(8,128)(2,1)} %param.26) | copy-start | bytes 196612
  9.5 155.3 %all-gather.9.cloned.1.call-start = ((), (), s32[]{:S(2)}) async-start(), calls=%async_computation.8 | async-start | bytes 5242880 | tf_op jit(solution)/shard_map/all_gather | solution.py:44
  10.0 183.4 %all-gather.15.cloned.1.call-start = ((), (), s32[]{:S(2)}) async-start(), calls=%async_computation.11 | async-start | bytes 1310720 | tf_op jit(solution)/shard_map/all_gather | solution.py:75
  86.4 217.2 %all-gather.21.cloned.1.call-start = ((), (), s32[]{:S(2)}) async-start(), calls=%async_computation.15 | async-start | bytes 2359296 | tf_op jit(solution)/shard_map/all_gather | solution.py:58
  86.9 216.7 %all-gather.23.cloned.1.call-start = ((), (), s32[]{:S(2)}) async-start(), calls=%async_computation.17 | async-start | bytes 5242880 | tf_op jit(solution)/shard_map/all_gather | solution.py:47
  87.7 387.2 %all-reduce.4.cloned.1.call-start = ((), (), s32[]{:S(2)}) async-start(), calls=%async_computation.13 | async-start | bytes 16777216 | tf_op jit(solution)/shard_map/psum | solution.py:126
  98.5 111.4 %copy-start.47 = (f32[1,1024]{1,0:T(1,128)}, f32[1,1024]{1,0:T(1,128)S(1)}, u32[]{:S(2)}) copy-start(f32[1,1024]{1,0:T(1,128)S(1)} %get-tuple-element.381) | copy-start | bytes 12292
  302.8 203.6 %all-gather.19.cloned.1.call-start = ((), (), s32[]{:S(2)}) async-start(), calls=%async_computation.14 | async-start | bytes 2359296 | tf_op jit(solution)/shard_map/all_gather | solution.py:54
  303.5 399.4 %all-reduce.8.cloned.1.call-start = ((), (), s32[]{:S(2)}) async-start(), calls=%async_computation.18 | async-start | bytes 16777216 | tf_op jit(solution)/shard_map/psum | solution.py:139
  531.3 1058.9 %all-reduce.6.cloned.1.call-start = ((), (), s32[]{:S(2)}) async-start(), calls=%async_computation.16 | async-start | bytes 8388608 | tf_op jit(solution)/shard_map/psum | solution.py:132
  875.1 272.1 %collective-permute-start = (f32[3072,1024]{1,0:T(8,128)}, f32[3072,1024]{1,0:T(8,128)S(1)}, u32[]{:S(2)}, u32[]{:S(2)}) collective-permute-start(f32[3072,1024]{1,0:T(8,128)} %pad_maximum_fusion), channel_id=1, source_target_pairs={{0,1},{1,0},{2,3},{3,2},{4,5},{5,4},{6,7},{7,6},{8,9},{9,8},{10,11... | collective-permute-start | bytes 37748744 | tf_op jit(solution)/shard_map/ppermute | solution.py:199
  1157.5 338.8 %collective-permute-start.1 = (f32[3072,1024]{1,0:T(8,128)}, f32[3072,1024]{1,0:T(8,128)}, u32[]{:S(2)}, u32[]{:S(2)}) collective-permute-start(f32[3072,1024]{1,0:T(8,128)} %fusion.74), channel_id=1, source_target_pairs={{0,2},{1,3},{2,0},{3,1},{4,6},{5,7},{6,4},{7,5},{8,10},{9,11},{10,... | collective-permute-start | bytes 37748744 | tf_op jit(solution)/shard_map/ppermute | solution.py:199
  1158.9 337.5 %copy-start.11 = (bf16[512,1024]{1,0:T(8,128)(2,1)S(1)}, bf16[512,1024]{1,0:T(8,128)(2,1)}, u32[]{:S(2)}) copy-start(bf16[512,1024]{1,0:T(8,128)(2,1)} %all-gather.17.cloned.1.call-done) | copy-start | bytes 3145732
  1158.9 337.5 %copy-start.13 = (bf16[512,1024]{1,0:T(8,128)(2,1)S(1)}, bf16[512,1024]{1,0:T(8,128)(2,1)}, u32[]{:S(2)}) copy-start(bf16[512,1024]{1,0:T(8,128)(2,1)} %all-gather.15.cloned.1.call-done) | copy-start | bytes 3145732
  1158.9 337.5 %copy-start.38 = (f32[3072]{0:T(1024)S(1)}, f32[3072]{0:T(1024)}, u32[]{:S(2)}) copy-start(f32[3072]{0:T(1024)} %copy-done.37) | copy-start | bytes 36868
  1158.9 337.5 %copy-start.40 = (f32[3072]{0:T(1024)S(1)}, f32[3072]{0:T(1024)}, u32[]{:S(2)}) copy-start(f32[3072]{0:T(1024)} %copy-done.39) | copy-start | bytes 36868
  1158.9 337.5 %copy-start.48 = (f32[1,1024]{1,0:T(1,128)S(1)}, f32[1,1024]{1,0:T(1,128)}, u32[]{:S(2)}) copy-start(f32[1,1024]{1,0:T(1,128)} %copy-done.47) | copy-start | bytes 12292
  1170.6 339.1 %copy-start.51 = (f32[1024]{0:T(1024)S(1)}, f32[1024]{0:T(1024)}, u32[]{:S(2)}) copy-start(f32[1024]{0:T(1024)} %get-tuple-element.316) | copy-start | bytes 12292
  1170.6 340.1 %copy-start.42 = (f32[3072]{0:T(1024)S(1)}, f32[3072]{0:T(1024)}, u32[]{:S(2)}) copy-start(f32[3072]{0:T(1024)} %copy-done.41) | copy-start | bytes 36868
  1170.6 429.6 %reduce-scatter.25.cloned.1.call-start = ((), (), s32[]{:S(2)}) async-start(), calls=%async_computation.26 | async-start | bytes 589824
  1540.9 73.0 %reduce-scatter.11.cloned.1.call-start = ((), (), s32[]{:S(2)}) async-start(), calls=%async_computation.19 | async-start | bytes 3538944 | tf_op jit(solution)/shard_map/reduce_scatter | solution.py:210
  1545.1 120.7 %reduce-scatter.21.cloned.1.call-start = ((), (), s32[]{:S(2)}) async-start(), calls=%async_computation.24 | async-start | bytes 4718592 | tf_op jit(solution)/shard_map/reduce_scatter | solution.py:214
  1555.3 161.6 %reduce-scatter.23.cloned.1.call-start = ((), (), s32[]{:S(2)}) async-start(), calls=%async_computation.25 | async-start | bytes 4718592 | tf_op jit(solution)/shard_map/reduce_scatter | solution.py:218
  1567.5 183.2 %reduce-scatter.19.cloned.1.call-start = ((), (), s32[]{:S(2)}) async-start(), calls=%async_computation.23 | async-start | bytes 1179648 | tf_op jit(solution)/shard_map/reduce_scatter | solution.py:217
  1573.2 211.2 %reduce-scatter.13.cloned.1.call-start = ((), (), s32[]{:S(2)}) async-start(), calls=%async_computation.20 | async-start | bytes 1179648 | tf_op jit(solution)/shard_map/reduce_scatter | solution.py:211
  1578.3 239.6 %reduce-scatter.15.cloned.1.call-start = ((), (), s32[]{:S(2)}) async-start(), calls=%async_computation.21 | async-start | bytes 1179648 | tf_op jit(solution)/shard_map/reduce_scatter | solution.py:212
  1584.4 267.1 %reduce-scatter.17.cloned.1.call-start = ((), (), s32[]{:S(2)}) async-start(), calls=%async_computation.22 | async-start | bytes 1179648 | tf_op jit(solution)/shard_map/reduce_scatter | solution.py:213
  (69 other events, 732.0 us)
Sparse Core Ops, SparseCore 0:
  9.8 46.4 all-gather.10
  58.0 25.2 all-gather.12
  85.1 25.4 all-gather.16
  112.3 52.4 all-gather.8
  167.0 26.3 all-gather.14
  194.9 30.5 all-gather.20
  227.3 51.4 all-gather.22
  302.9 171.9 all-reduce.3
  476.5 29.8 all-gather.18
  531.5 171.4 all-reduce.7
  1170.7 171.4 all-reduce.5
  1541.0 31.9 reduce-scatter.24
  1575.3 38.5 reduce-scatter.10
  1616.6 49.1 reduce-scatter.20
  1668.5 48.3 reduce-scatter.22
  1719.6 31.0 reduce-scatter.18
  1753.4 30.9 reduce-scatter.12
  1787.1 30.7 reduce-scatter.14
  1820.7 30.7 reduce-scatter.16
